TPU v7x, 32 devices: a whole 2x2x4 slice. The times are simulated.
32 devices in a mesh: fsdp: 8 (over y, x, core), rep: 4 (over z).
Axes of the slice: x: 2, y: 2, z: 4, core: 2. Of those that a mesh axis runs over, the one named last changes fastest.
Arguments:
- tokens: bfloat16 [65536, 768], P(('fsdp', 'rep')), may hold values from -6 to 6
- segment_ids: int32 [65536], P(('fsdp', 'rep')), may hold values from -1 to 8, as said below
- cotangent: bfloat16 [65536, 768], P(('fsdp', 'rep')), may hold values from -8 to 8
- norm_params: bfloat16 [4, 768], P(None, 'fsdp')
- qkv_weight: bfloat16 [768, 2304], P(None, 'fsdp'), may hold values from -0.21875 to 0.21875
- proj_weight: bfloat16 [768, 768], P(None, 'fsdp'), may hold values from -1.25 to 1.25
- up_weight: bfloat16 [768, 3072], P(None, 'fsdp'), may hold values from -0.21875 to 0.21875
- down_weight: bfloat16 [3072, 768], P(None, 'fsdp'), may hold values from -0.109375 to 0.109375
- target_norms: float32 [4, 768], P(None, 'fsdp'), may hold values from -3 to 3
- target_qkv: float32 [768, 2304], P(None, 'fsdp'), may hold values from -0.21875 to 0.21875
- target_proj: float32 [768, 768], P(None, 'fsdp'), may hold values from -1.25 to 1.25
- target_up: float32 [768, 3072], P(None, 'fsdp'), may hold values from -0.21875 to 0.21875
- target_down: float32 [3072, 768], P(None, 'fsdp'), may hold values from -0.109375 to 0.109375
Outputs:
- block_output: bfloat16 [65536, 768], P(('fsdp', 'rep'))
- input_grad: bfloat16 [65536, 768], P(('fsdp', 'rep'))
- norm_grad: float32 [4, 768], P(None, 'fsdp')
- qkv_grad: float32 [768, 2304], P(None, 'fsdp')
- proj_grad: float32 [768, 768], P(None, 'fsdp')
- up_grad: float32 [768, 3072], P(None, 'fsdp')
- down_grad: float32 [3072, 768], P(None, 'fsdp')
- new_target_norms: float32 [4, 768], P(None, 'fsdp')
- new_target_qkv: float32 [768, 2304], P(None, 'fsdp')
- new_target_proj: float32 [768, 768], P(None, 'fsdp')
- new_target_up: float32 [768, 3072], P(None, 'fsdp')
- new_target_down: float32 [3072, 768], P(None, 'fsdp')
Inputs may be any that keep to these rules, and one draw needn't show every extreme that they name: `segment_ids`: in each packed row of 1024 slots, images fill consecutive slots from the row's start with ids 0, 1, 2, ... in order; each image has 98 to 196 slots and one image of each row has exactly 196; the remaining slots at the row's end are -1. In the first packed row all images except the one of 196 slots have exactly 98 slots.
All inputs are finite; a program needn't handle non-finite values.
Results may differ from a plain program's by a relative error of at most 0.014.
Values may be sent and summed in bfloat16 or wider, within the bound.
No kernel may reach another device: no remote copies, remote signals or barrier semaphores. Data moves between devices by JAX's collectives and lax.ppermute only.
A program may use at most 256 MiB of HBM per device.

v0:
```python
import jax
import jax.numpy as jnp
from jax import lax
from jax.sharding import PartitionSpec as P

HEAD = 64
ROW_LEN = 1024
layer_eps = 1e-06
ema_rate = 0.75


def layer_norm(values, gain, shift):
    center = values - jnp.mean(values, axis=-1, keepdims=True)
    spread = jnp.mean(center * center, axis=-1, keepdims=True)
    return center * lax.rsqrt(spread + layer_eps) * gain + shift


def gelu_exact(values):
    return jax.nn.gelu(values, approximate=False)


def product(left, right):
    return jnp.dot(left, right, preferred_element_type=jnp.float32)


def outer_sum(left, right):
    return lax.dot_general(
        left, right, (((0,), (0,)), ((), ())), preferred_element_type=jnp.float32
    )


def against(left, right):
    return lax.dot_general(
        left, right, (((1,), (1,)), ((), ())), preferred_element_type=jnp.float32
    )


def split_heads(matrix, rows):
    count, width = matrix.shape
    heads = width // HEAD
    shaped = matrix.reshape(rows, count // rows, heads, HEAD)
    return shaped.transpose(0, 2, 1, 3).reshape(rows * heads, count // rows, HEAD)


def merge_heads(stacked, rows):
    items, length, size = stacked.shape
    heads = items // rows
    shaped = stacked.reshape(rows, heads, length, size).transpose(0, 2, 1, 3)
    return shaped.reshape(rows * length, heads * size)


def masked_scores(query, keyset, segment):
    same = segment[:, None] == segment[None, :]
    return jnp.where(same, against(query, keyset) * 0.125, -1e30)


def head_forward(item):
    query, keyset, value, segment = item
    scores = masked_scores(query, keyset, segment)
    top = jnp.max(scores, axis=1, keepdims=True)
    expo = jnp.exp(scores - top)
    total = jnp.sum(expo, axis=1, keepdims=True)
    weights = (expo / total).astype(jnp.bfloat16)
    return (product(weights, value), top, total)


def head_backward(item):
    query, keyset, value, segment, top, total, grad_head = item
    scores = masked_scores(query, keyset, segment)
    probs = jnp.exp(scores - top) / total
    grad_probs = against(grad_head, value)
    center = jnp.sum(probs * grad_probs, axis=1, keepdims=True)
    grad_scores = (probs * (grad_probs - center)).astype(jnp.bfloat16)
    grad_query = product(grad_scores, keyset) * 0.125
    grad_key = outer_sum(grad_scores, query) * 0.125
    grad_value = outer_sum(probs.astype(jnp.bfloat16), grad_head)
    return (grad_query, grad_key, grad_value)


def per_device(
    tokens,
    segment_ids,
    cotangent,
    norm_params,
    qkv_weight,
    proj_weight,
    up_weight,
    down_weight,
    target_norms,
    target_qkv,
    target_proj,
    target_up,
    target_down,
):
    norms, w_qkv, w_proj, w_up, w_down = (
        lax.all_gather(norm_params, "fsdp", axis=1, tiled=True),
        lax.all_gather(qkv_weight, "fsdp", axis=1, tiled=True),
        lax.all_gather(proj_weight, "fsdp", axis=1, tiled=True),
        lax.all_gather(up_weight, "fsdp", axis=1, tiled=True),
        lax.all_gather(down_weight, "fsdp", axis=1, tiled=True),
    )
    gains = norms.astype(jnp.float32)
    count, width = tokens.shape
    rows = count // ROW_LEN
    heads = width // HEAD
    inputs = tokens.astype(jnp.float32)
    valid = (segment_ids >= 0).astype(jnp.float32)[:, None]
    first = layer_norm(inputs, gains[0], gains[1]).astype(jnp.bfloat16)
    qkv = product(first, w_qkv).astype(jnp.bfloat16)
    query = split_heads(qkv[:, :width], rows)
    keyset = split_heads(qkv[:, width : 2 * width], rows)
    value = split_heads(qkv[:, 2 * width :], rows)
    segments = jnp.repeat(segment_ids.reshape(rows, ROW_LEN), heads, axis=0)
    head_out, tops, totals = lax.map(head_forward, (query, keyset, value, segments))
    attended = merge_heads(head_out, rows).astype(jnp.bfloat16)
    middle = inputs + product(attended, w_proj)
    second = layer_norm(middle, gains[2], gains[3]).astype(jnp.bfloat16)
    upper = product(second, w_up)
    activated = gelu_exact(upper).astype(jnp.bfloat16)
    final = middle + product(activated, w_down)
    block_output = (final * valid).astype(jnp.bfloat16)
    norms, w_qkv, w_proj, w_up, w_down = (
        lax.all_gather(norm_params, "fsdp", axis=1, tiled=True),
        lax.all_gather(qkv_weight, "fsdp", axis=1, tiled=True),
        lax.all_gather(proj_weight, "fsdp", axis=1, tiled=True),
        lax.all_gather(up_weight, "fsdp", axis=1, tiled=True),
        lax.all_gather(down_weight, "fsdp", axis=1, tiled=True),
    )
    gains = norms.astype(jnp.float32)
    grad_out = (cotangent.astype(jnp.float32) * valid).astype(jnp.bfloat16)
    grad_down = outer_sum(activated, grad_out)
    grad_act = against(grad_out, w_down)
    gelu_back = jax.vjp(gelu_exact, upper)[1]
    grad_upper = gelu_back(grad_act)[0].astype(jnp.bfloat16)
    grad_up = outer_sum(second, grad_upper)
    grad_second = against(grad_upper, w_up)
    second_back = jax.vjp(layer_norm, middle, gains[2], gains[3])[1]
    grad_mid_norm, grad_gain_two, grad_shift_two = second_back(grad_second)
    grad_middle = grad_out.astype(jnp.float32) + grad_mid_norm
    grad_branch = grad_middle.astype(jnp.bfloat16)
    grad_proj = outer_sum(attended, grad_branch)
    grad_attended = against(grad_branch, w_proj).astype(jnp.bfloat16)
    grad_heads = split_heads(grad_attended, rows)
    grad_query, grad_key, grad_value = lax.map(
        head_backward, (query, keyset, value, segments, tops, totals, grad_heads)
    )
    grad_qkv = jnp.concatenate(
        [merge_heads(grad_query, rows), merge_heads(grad_key, rows), merge_heads(grad_value, rows)],
        axis=1,
    ).astype(jnp.bfloat16)
    grad_wqkv = outer_sum(first, grad_qkv)
    grad_first = against(grad_qkv, w_qkv)
    first_back = jax.vjp(layer_norm, inputs, gains[0], gains[1])[1]
    grad_in_norm, grad_gain_one, grad_shift_one = first_back(grad_first)
    input_grad = (grad_middle + grad_in_norm).astype(jnp.bfloat16)
    grad_norms = jnp.stack([grad_gain_one, grad_shift_one, grad_gain_two, grad_shift_two])
    owned = (
        lax.psum_scatter(grad_norms, "fsdp", scatter_dimension=1, tiled=True),
        lax.psum_scatter(grad_wqkv, "fsdp", scatter_dimension=1, tiled=True),
        lax.psum_scatter(grad_proj, "fsdp", scatter_dimension=1, tiled=True),
        lax.psum_scatter(grad_up, "fsdp", scatter_dimension=1, tiled=True),
        lax.psum_scatter(grad_down, "fsdp", scatter_dimension=1, tiled=True),
    )
    summed = (
        lax.psum(owned[0].astype(jnp.bfloat16), "rep").astype(jnp.float32),
        lax.psum(owned[1].astype(jnp.bfloat16), "rep").astype(jnp.float32),
        lax.psum(owned[2].astype(jnp.bfloat16), "rep").astype(jnp.float32),
        lax.psum(owned[3].astype(jnp.bfloat16), "rep").astype(jnp.float32),
        lax.psum(owned[4].astype(jnp.bfloat16), "rep").astype(jnp.float32),
    )
    keep_rate = 1.0 - ema_rate
    new_norms = ema_rate * target_norms + keep_rate * norm_params.astype(jnp.float32)
    new_qkv = ema_rate * target_qkv + keep_rate * qkv_weight.astype(jnp.float32)
    new_proj = ema_rate * target_proj + keep_rate * proj_weight.astype(jnp.float32)
    new_up = ema_rate * target_up + keep_rate * up_weight.astype(jnp.float32)
    new_down = ema_rate * target_down + keep_rate * down_weight.astype(jnp.float32)
    return (
        block_output,
        input_grad,
        summed[0],
        summed[1],
        summed[2],
        summed[3],
        summed[4],
        new_norms,
        new_qkv,
        new_proj,
        new_up,
        new_down,
    )


def solution(mesh):
    return jax.shard_map(
        per_device,
        mesh=mesh,
        in_specs=(
            P(("fsdp", "rep"), None),
            P(("fsdp", "rep")),
            P(("fsdp", "rep"), None),
            P(None, "fsdp"),
            P(None, "fsdp"),
            P(None, "fsdp"),
            P(None, "fsdp"),
            P(None, "fsdp"),
            P(None, "fsdp"),
            P(None, "fsdp"),
            P(None, "fsdp"),
            P(None, "fsdp"),
            P(None, "fsdp"),
        ),
        out_specs=(
            P(("fsdp", "rep"), None),
            P(("fsdp", "rep"), None),
            P(None, "fsdp"),
            P(None, "fsdp"),
            P(None, "fsdp"),
            P(None, "fsdp"),
            P(None, "fsdp"),
            P(None, "fsdp"),
            P(None, "fsdp"),
            P(None, "fsdp"),
            P(None, "fsdp"),
            P(None, "fsdp"),
        ),
        check_vma=False,
    )
```

profile of v0, /device:TPU:0, one launch (start us, length us, event | category | flops | bytes accessed | tf_op | source)
XLA Modules:
  0.0 1168.2 jit_solution(18009675124772495406)
XLA Ops:
  16.7 10.4 all-gather
  32.0 14.6 %all-gather.6.cloned.1.call-done = bf16[768,2304]{0,1:T(8,128)(2,1)} async-done(((bf16[768,288]{0,1:T(8,128)(2,1)}), bf16[768,2304]{0,1:T(8,128)(2,1)}) %all-gather.6.cloned.1.call-update) | async-done | bytes 3538960 | tf_op jit(solution)/shard_map/all_gather | solution.py:97
  46.6 10.6 convolution_convert_fusion
  65.9 6.1 reshape.164
  72.0 9.8 copy.144
  86.6 6.1 reshape.166
  92.7 9.9 copy.145
  107.3 6.1 reshape.168
  113.4 9.7 copy.146
  125.2 152.9 %while.28 = (s32[]{:T(128)}, bf16[24,1024,64]{1,2,0:T(8,128)(2,1)}, f32[24,1024,1]{1,2,0:T(1,128)}, f32[24,1024,1]{1,2,0:T(1,128)}, s32[24,1024]{1,0:T(8,128)S(1...) while((s32[]{:T(128)}, bf16[24,1024,64]{1,2,0:T(8,128)(2,1)}, ...), condition=%wide.region_5.6_spmd, body=%wide.region_2.5_spmd.sunk | while | flops 284162048 | bytes 13699681 | solution.py:114
  278.2 5.2 copy.125
  296.4 67.5 %multiply_convert_fusion.1 = (bf16[2048,3072]{1,0:T(8,128)(2,1)}, f32[2048,3072]{1,0:T(8,128)}, f32[2048,3072]{1,0:T(8,128)}) fusion(bf16[768,3072]{1,0:T(8,128)(2,1)} %all-gather.10.cloned.1.call-done, bf16[2048,768]{0,1:T(8,128)(2,1)} %add_convert_fusion.4.clone.4), kind=kOutput, calls=%fused_computation.61 | convolution fusion | flops 10072621056 | bytes 70778880 | tf_op jit(solution)/shard_map/dot_general | solution.py:23
  364.0 27.9 %add_convert_fusion = bf16[2048,3072]{1,0:T(8,128)(2,1)} fusion(f32[2048,3072]{1,0:T(8,128)} %get-tuple-element.291, f32[2048,3072]{1,0:T(8,128)} %get-tuple-element.305, bf16[3072,768]{0,1:T(8,128)(2,1)} %all-gather.12.cloned.1.call-done, bf16[2048,768]{0,1:T(8,128)(2,1)S(1)} %copy-done.6, f32[2048]{0:T(1024)S(1)} %copy-done.21), kind=kOutput, calls=%fused_computation.60 | convolution fusion | flops 9756475392 | bytes 70787072 | tf_op jit(solution)/shard_map/dot_general | solution.py:33
  391.9 16.6 %fusion.79 = (f32[768]{0:T(1024)}, f32[2048,768]{1,0:T(8,128)}) fusion(bf16[2048,3072]{1,0:T(8,128)(2,1)} %add_convert_fusion, bf16[768,3072]{1,0:T(8,128)(2,1)} %all-gather.10.cloned.1.call-done), kind=kOutput, calls=%fused_computation.135 | convolution fusion | flops 9665248256 | bytes 23596032 | tf_op jit(solution)/shard_map/dot_general | solution.py:33
  408.4 6.7 copy.128
  415.2 6.7 multiply_reduce_fusion.1
  433.3 5.3 convolution_convert_fusion.1
  445.7 9.8 copy.149
  460.1 320.7 %while.29 = (s32[]{:T(128)}, bf16[24,1024,64]{1,2,0:T(8,128)(2,1)S(1)}, bf16[24,1024,64]{1,2,0:T(8,128)(2,1)}, bf16[24,1024,64]{1,2,0:T(8,128)(2,1)}, s32[24,102...) while((s32[]{:T(128)}, ...), condition=%wide.region_12.13_spmd, body=%wide.region_10.12_spmd.sunk | while | flops 682753024 | bytes 34133116 | solution.py:144
  789.4 5.3 copy.137
  800.6 10.0 fusion.70
  811.4 17.0 %fusion.73 = f32[768,3072]{1,0:T(8,128)} fusion(bf16[2048,3072]{1,0:T(8,128)(2,1)} %add_convert_fusion, f32[2048,768]{0,1:T(8,128)} %copy-done.2, f32[768]{0:T(1024)S(1)} %copy-done.35, f32[768]{0:T(1024)S(1)} %copy-done.33, f32[2048]{0:T(1024)S(1)} %copy-done.20, f32[2048]{0:T(1024)S(1)} %copy-done.15), kind=kOutput, calls=%fused_computation.130 | convolution fusion | flops 9671540736 | bytes 28334080 | tf_op jit(solution)/shard_map/dot_general | solution.py:27
  828.5 16.1 %fusion.66 = f32[3072,768]{0,1:T(8,128)} fusion(bf16[2048,3072]{1,0:T(8,128)(2,1)} %get-tuple-element.290, bf16[2048,768]{0,1:T(8,128)(2,1)} %copy.127, f32[2048]{0:T(1024)S(1)} %copy-done.21), kind=kOutput, calls=%fused_computation.102 | convolution fusion | flops 9668395008 | bytes 25174016 | tf_op jit(solution)/shard_map/dot_general | solution.py:27
  854.1 12.1 %fusion.80 = (f32[768]{0:T(1024)S(1)}, f32[2048,768]{1,0:T(8,128)}) fusion(bf16[2048,2304]{0,1:T(8,128)(2,1)} %copy-done.12, bf16[768,2304]{0,1:T(8,128)(2,1)S(1)} %copy-done.43), kind=kOutput, calls=%fused_computation.136 | convolution fusion | flops 7249329152 | bytes 19270656 | tf_op jit(solution)/shard_map/dot_general | solution.py:33
  866.1 6.6 copy.138
  882.0 10.0 add_convert_fusion.1
  900.6 55.7 %reduce-scatter.12.cloned.1.call-done = f32[768,384]{1,0:T(8,128)} async-done(((f32[768,3072]{1,0:T(8,128)}), f32[768,384]{1,0:T(8,128)}) %reduce-scatter.12.cloned.1.call-update) | async-done | bytes 1179664 | tf_op jit(solution)/shard_map/reduce_scatter | solution.py:161
  958.5 77.9 %reduce-scatter.14.cloned.1.call-done = f32[3072,96]{0,1:T(8,128)} async-done(((f32[3072,768]{0,1:T(8,128)}), f32[3072,96]{0,1:T(8,128)}) %reduce-scatter.14.cloned.1.call-update) | async-done | bytes 1179664 | tf_op jit(solution)/shard_map/reduce_scatter | solution.py:162
  1038.5 17.1 %multiply_convert_fusion.3 = bf16[2048,768]{0,1:T(8,128)(2,1)S(1)} fusion(f32[2048,768]{0,1:T(8,128)} %copy-done.2, bf16[2048,3072]{1,0:T(8,128)(2,1)} %get-tuple-element.290, bf16[3072,768]{0,1:T(8,128)(2,1)} %all-gather.12.cloned.1.call-done, f32[2048]{0:T(1024)S(1)} %copy-done.21), kind=kOutput, calls=%fused_computation.97 | convolution fusion | flops 9668395008 | bytes 26746880 | tf_op jit(solution)/shard_map/dot_general | solution.py:23
  1058.4 14.9 %reduce-scatter.16.cloned.1.call-done = f32[96,4]{1,0:T(8,128)} async-done(((f32[768,4]{1,0:T(8,128)}), f32[96,4]{1,0:T(8,128)}) %reduce-scatter.16.cloned.1.call-update) | async-done | bytes 1552
  1074.2 11.8 %psum.35 = bf16[4,96]{1,0:T(4,128)(2,1)S(1)} all-reduce(bf16[4,96]{1,0:T(4,128)(2,1)S(1)} %copy.152), channel_id=1, replica_groups=mesh['fsdp'=8,'rep'=4] {'rep'}, use_global_device_ids=true, to_apply=%region_20.21 | all-reduce | flops 384 | bytes 1536 | tf_op jit(solution)/shard_map/psum | solution.py:165
  1086.5 66.5 %all-reduce.3.cloned.1.call-done = (bf16[768,288]{0,1:T(8,128)(2,1)}, bf16[768,96]{0,1:T(8,128)(2,1)}, bf16[768,384]{1,0:T(8,128)(2,1)}, bf16[3072,96]{0,1:T(8,128)(2,1)}) async-done(((bf16[768,288]{0,1:T(8,128)(2,1)}, bf16[768,96]{0,1:T(8,128)(2,1)}, bf16[768,384]{1,0:T(8,128)(2,1)}, bf16[3072,96]{0,1:T(8,128)(2,1)}), (bf16[768,288]{0,1:T(8,128)(2,1)}, bf16[768,96]{0,1:T(8,128)(2,1)}, ...) | async-done | bytes 1769488 | tf_op jit(solution)/shard_map/psum | solution.py:166
  (501 shorter events, 601.4 us)
Async XLA Ops:
  7.2 39.4 %all-gather.6.cloned.1.call-start = ((), (), s32[]{:S(2)}) async-start(), calls=%async_computation.5 | async-start | bytes 3981312 | tf_op jit(solution)/shard_map/all_gather | solution.py:97
  7.9 278.2 %all-gather.8.cloned.1.call-start = ((), (), s32[]{:S(2)}) async-start(), calls=%async_computation.6 | async-start | bytes 1327104 | tf_op jit(solution)/shard_map/all_gather | solution.py:98
  8.7 287.7 %all-gather.10.cloned.1.call-start = ((), (), s32[]{:S(2)}) async-start(), calls=%async_computation.7 | async-start | bytes 5308416 | tf_op jit(solution)/shard_map/all_gather | solution.py:99
  9.4 354.5 %all-gather.12.cloned.1.call-start = ((), (), s32[]{:S(2)}) async-start(), calls=%async_computation.8 | async-start | bytes 5308416 | tf_op jit(solution)/shard_map/all_gather | solution.py:100
  10.0 887.0 %reduce-scatter.10.cloned.1.call-start = ((), (), s32[]{:S(2)}) async-start(), calls=%async_computation.10 | async-start | bytes 2654208 | tf_op jit(solution)/shard_map/reduce_scatter | solution.py:160
  15.2 270.8 %copy-start = (bf16[2048,768]{0,1:T(8,128)(2,1)}, bf16[2048,768]{0,1:T(8,128)(2,1)S(1)}, u32[]{:S(2)}) copy-start(bf16[2048,768]{0,1:T(8,128)(2,1)S(1)} %copy.114) | copy-start | bytes 9437188
  15.8 41.5 %copy-start.16 = (f32[2048]{0:T(1024)}, f32[2048]{0:T(1024)S(1)}, u32[]{:S(2)}) copy-start(f32[2048]{0:T(1024)S(1)} %broadcast_multiply_fusion.1) | copy-start | bytes 24580
  16.6 10.5 copy-start.24
  16.6 40.6 %copy-start.28 = (f32[2048]{0:T(1024)}, f32[2048]{0:T(1024)S(1)}, u32[]{:S(2)}) copy-start(f32[2048]{0:T(1024)S(1)} %fusion.68) | copy-start | bytes 24580
  27.2 30.1 %copy-start.30 = (f32[768]{0:T(1024)}, f32[768]{0:T(1024)S(1)}, u32[]{:S(2)}) copy-start(f32[768]{0:T(1024)S(1)} %get-tuple-element.245) | copy-start | bytes 9220
  27.2 30.1 %copy-start.37 = (f32[768]{0:T(1024)}, f32[768]{0:T(1024)S(1)}, u32[]{:S(2)}) copy-start(f32[768]{0:T(1024)S(1)} %get-tuple-element.244) | copy-start | bytes 9220
  27.2 265.6 %copy-start.32 = (f32[768]{0:T(1024)}, f32[768]{0:T(1024)S(1)}, u32[]{:S(2)}) copy-start(f32[768]{0:T(1024)S(1)} %get-tuple-element.242) | copy-start | bytes 9220
  27.2 265.6 %copy-start.34 = (f32[768]{0:T(1024)}, f32[768]{0:T(1024)S(1)}, u32[]{:S(2)}) copy-start(f32[768]{0:T(1024)S(1)} %get-tuple-element.243) | copy-start | bytes 9220
  278.2 7.9 copy-start.18
  296.4 67.5 %copy-start.6 = (bf16[2048,768]{0,1:T(8,128)(2,1)S(1)}, bf16[2048,768]{0,1:T(8,128)(2,1)}, u32[]{:S(2)}) copy-start(bf16[2048,768]{0,1:T(8,128)(2,1)} %copy.127) | copy-start | bytes 9437188
  296.4 67.5 %copy-start.21 = (f32[2048]{0:T(1024)S(1)}, f32[2048]{0:T(1024)}, u32[]{:S(2)}) copy-start(f32[2048]{0:T(1024)} %compare_convert_fusion) | copy-start | bytes 24580
  408.4 6.7 copy-start.15
  408.4 6.7 copy-start.20
  408.4 6.7 copy-start.33
  408.4 13.5 %slice-start = ((s8[6291456]{0:T(1024)(128)(4,1)}), s8[2097152]{0:T(1024)(128)(4,1)S(1)}, s32[]{:S(2)}) async-start(s8[6291456]{0:T(1024)(128)(4,1)} %bitcast.182), calls=%async_computation.15 | async-start | bytes 4194304
  415.2 6.8 copy-start.27
  415.2 6.8 slice-start.1
  415.2 7.7 copy-start.4
  455.5 443.1 %reduce-scatter.8.cloned.1.call-start = ((), (), s32[]{:S(2)}) async-start(), calls=%async_computation.9 | async-start | bytes 7962624 | tf_op jit(solution)/shard_map/reduce_scatter | solution.py:159
  810.7 145.6 %reduce-scatter.12.cloned.1.call-start = ((), (), s32[]{:S(2)}) async-start(), calls=%async_computation.11 | async-start | bytes 10616832 | tf_op jit(solution)/shard_map/reduce_scatter | solution.py:161
  828.4 207.9 %reduce-scatter.14.cloned.1.call-start = ((), (), s32[]{:S(2)}) async-start(), calls=%async_computation.12 | async-start | bytes 10616832 | tf_op jit(solution)/shard_map/reduce_scatter | solution.py:162
  844.6 228.7 %reduce-scatter.16.cloned.1.call-start = ((), (), s32[]{:S(2)}) async-start(), calls=%async_computation.13 | async-start | bytes 442368
  845.2 7.6 copy-start.10
  845.2 7.6 copy-start.11
  845.2 8.8 copy-start.43
  876.8 5.2 copy-start.23
  881.7 271.3 %all-reduce.3.cloned.1.call-start = ((), (), s32[]{:S(2)}) async-start(), calls=%async_computation.14 | async-start | bytes 3538944 | tf_op jit(solution)/shard_map/psum | solution.py:166
  (24 other events, 75.4 us)
Sparse Core Ops, SparseCore 0:
  9.9 36.6 all-gather.5
  48.5 24.0 all-gather.7
  74.5 39.7 all-gather.9
  116.0 38.9 all-gather.11
  455.6 42.4 reduce-scatter.9
  810.8 65.4 reduce-scatter.7
  879.8 76.4 reduce-scatter.11
  959.8 76.4 reduce-scatter.13
  1039.4 33.8 reduce-scatter.15
  1076.4 76.5 all-reduce.2
where the time goes:
time: 1190 us; the launch traced here: 1170 us
  matrix products  579 us (49%)
  waiting for transfers between devices  232 us (19%)
  local copies, waits for them, and re-layouts  206 us (17%)
  other arithmetic  111 us (9%)
  blocking collectives  22.2 us (2%)
  between operations  15.3 us (1%)
    dot_general x76, matrix products, against(): lax.dot_general(left, right, (((1,), (1,)), ((), ())), preferred_element_...  211 us
    dot_general x52, matrix products, product(): return jnp.dot(left, right, preferred_element_type=jnp.float32)  206 us
    dot_general x52, matrix products, outer_sum(): lax.dot_general(left, right, (((0,), (0,)), ((), ())), preferred_element_...  162 us
    reduce_scatter x1, waiting for transfers between devices, per_device(): lax.psum_scatter(grad_down, 'fsdp', scatter_dimension=1, tiled=True)  77.9 us
    psum x1, waiting for transfers between devices, per_device(): lax.psum(owned[1].astype(jnp.bfloat16), 'rep').astype(jnp.float32)  66.5 us
    reduce_scatter x1, waiting for transfers between devices, per_device(): lax.psum_scatter(grad_up, 'fsdp', scatter_dimension=1, tiled=True)  55.7 us
    reshape x4, local copies, waits for them, and re-layouts, split_heads(): shaped.transpose(0, 2, 1, 3).reshape(rows * heads, count // rows, HEAD)  39.2 us
    unnamed x104, local copies, waits for them, and re-layouts  35.3 us
  transfers between devices with their start and end apart: 10, of which 5 were waited for; matrix products, arithmetic and copies ran while one was open for 68% of the time, Pallas kernels for 0%

commit v1 on v0

--- a/solution.py
+++ b/solution.py
@@ -163,7 +163,7 @@
     )
     summed = (
         lax.psum(owned[0].astype(jnp.bfloat16), "rep").astype(jnp.float32),
-        lax.psum(owned[1].astype(jnp.bfloat16), "rep").astype(jnp.float32),
+        jnp.sum(lax.all_gather(owned[1].astype(jnp.bfloat16), "rep"), axis=0).astype(jnp.float32),
         lax.psum(owned[2].astype(jnp.bfloat16), "rep").astype(jnp.float32),
         lax.psum(owned[3].astype(jnp.bfloat16), "rep").astype(jnp.float32),
         lax.psum(owned[4].astype(jnp.bfloat16), "rep").astype(jnp.float32),

time: 1190 us -> 1270 us (1.067)
  waiting for transfers between devices: 232 us -> 290 us
  matrix products: 579 us -> 599 us
    all_gather x0 -> x1, waiting for transfers between devices: none -> 29.1 us  [per_device(): lax.all_gather(owned[1].astype(jnp.bfloat16), 'rep')]
    reduce_scatter x1, waiting for transfers between devices: 55.7 us -> 78.4 us  [per_device(): lax.psum_scatter(grad_up, 'fsdp', scatter_dimension=1, tiled=True)]
    dot_general x52, matrix products: 206 us -> 221 us  [product(): return jnp.dot(left, right, preferred_element_type=jnp.float32)]
    unnamed x104 -> x102, local copies, waits for them, and re-layouts: 35.3 us -> 35.6 us
  transfers between devices with their start and end apart: 10 -> 11, of which waited for: 5 -> 7; matrix products, arithmetic and copies ran while one was open for 68% -> 36% of each run, Pallas kernels for 0% -> 0%
where the time goes in v1:
time: 1270 us; the launch traced here: 1250 us
  matrix products  599 us (47%)
  waiting for transfers between devices  290 us (23%)
  local copies, waits for them, and re-layouts  213 us (17%)
  other arithmetic  111 us (9%)
  blocking collectives  22.2 us (2%)
  between operations  15 us (1%)
    dot_general x52, matrix products, product(): return jnp.dot(left, right, preferred_element_type=jnp.float32)  221 us
    dot_general x76, matrix products, against(): lax.dot_general(left, right, (((1,), (1,)), ((), ())), preferred_element_...  211 us
    dot_general x52, matrix products, outer_sum(): lax.dot_general(left, right, (((0,), (0,)), ((), ())), preferred_element_...  166 us
    reduce_scatter x1, waiting for transfers between devices, per_device(): lax.psum_scatter(grad_up, 'fsdp', scatter_dimension=1, tiled=True)  78.4 us
    reduce_scatter x1, waiting for transfers between devices, per_device(): lax.psum_scatter(grad_down, 'fsdp', scatter_dimension=1, tiled=True)  77.9 us
    psum x1, waiting for transfers between devices, per_device(): lax.psum(owned[2].astype(jnp.bfloat16), 'rep').astype(jnp.float32)  56.7 us
    reshape x4, local copies, waits for them, and re-layouts, split_heads(): shaped.transpose(0, 2, 1, 3).reshape(rows * heads, count // rows, HEAD)  39.1 us
    unnamed x102, local copies, waits for them, and re-layouts  35.6 us
  transfers between devices with their start and end apart: 11, of which 7 were waited for; matrix products, arithmetic and copies ran while one was open for 36% of the time, Pallas kernels for 0%

profile of v1, /device:TPU:0, one launch (start us, length us, event | category | flops | bytes accessed | tf_op | source)
XLA Modules:
  0.0 1252.7 jit_solution(18219589154975229707)
XLA Ops:
  17.2 10.4 all-gather.1
  32.5 14.1 %all-gather.8.cloned.1.call-done = bf16[768,2304]{0,1:T(8,128)(2,1)} async-done(((bf16[768,288]{0,1:T(8,128)(2,1)}), bf16[768,2304]{0,1:T(8,128)(2,1)}) %all-gather.8.cloned.1.call-update) | async-done | bytes 3538960 | tf_op jit(solution)/shard_map/all_gather | solution.py:97
  46.6 10.6 convolution_convert_fusion
  65.8 6.1 reshape.164
  71.9 9.8 copy.144
  86.4 6.1 reshape.166
  92.6 9.8 copy.145
  107.0 6.1 reshape.168
  113.1 9.7 copy.146
  124.9 153.1 %while.28 = (s32[]{:T(128)}, bf16[24,1024,64]{1,2,0:T(8,128)(2,1)}, f32[24,1024,1]{1,2,0:T(1,128)}, f32[24,1024,1]{1,2,0:T(1,128)}, s32[24,1024]{1,0:T(8,128)S(1...) while((s32[]{:T(128)}, bf16[24,1024,64]{1,2,0:T(8,128)(2,1)}, ...), condition=%wide.region_5.6_spmd, body=%wide.region_2.5_spmd.sunk | while | flops 284162048 | bytes 13699681 | solution.py:114
  296.2 67.6 %multiply_convert_fusion.1 = (bf16[2048,3072]{1,0:T(8,128)(2,1)}, f32[2048,3072]{1,0:T(8,128)}, f32[2048,3072]{1,0:T(8,128)}) fusion(bf16[768,3072]{1,0:T(8,128)(2,1)} %all-gather.12.cloned.1.call-done, bf16[2048,768]{0,1:T(8,128)(2,1)} %add_convert_fusion.4.clone.4), kind=kOutput, calls=%fused_computation.61 | convolution fusion | flops 10072621056 | bytes 70778880 | tf_op jit(solution)/shard_map/dot_general | solution.py:23
  363.9 27.9 %add_convert_fusion = bf16[2048,3072]{1,0:T(8,128)(2,1)} fusion(f32[2048,3072]{1,0:T(8,128)} %get-tuple-element.290, f32[2048,3072]{1,0:T(8,128)} %get-tuple-element.304, bf16[3072,768]{0,1:T(8,128)(2,1)} %all-gather.14.cloned.1.call-done, bf16[2048,768]{0,1:T(8,128)(2,1)S(1)} %copy-done.6, f32[2048]{0:T(1024)S(1)} %copy-done.21), kind=kOutput, calls=%fused_computation.60 | convolution fusion | flops 9756475392 | bytes 70787072 | tf_op jit(solution)/shard_map/dot_general | solution.py:33
  391.8 16.5 %fusion.79 = (f32[768]{0:T(1024)}, f32[2048,768]{1,0:T(8,128)}) fusion(bf16[2048,3072]{1,0:T(8,128)(2,1)} %add_convert_fusion, bf16[768,3072]{1,0:T(8,128)(2,1)} %all-gather.12.cloned.1.call-done), kind=kOutput, calls=%fused_computation.135 | convolution fusion | flops 9665248256 | bytes 23596032 | tf_op jit(solution)/shard_map/dot_general | solution.py:33
  408.4 6.7 copy.128
  415.1 6.4 multiply_reduce_fusion.1
  441.1 9.7 copy.149
  457.0 336.0 %while.29 = (s32[]{:T(128)}, bf16[24,1024,64]{1,2,0:T(8,128)(2,1)}, bf16[24,1024,64]{1,2,0:T(8,128)(2,1)}, bf16[24,1024,64]{1,2,0:T(8,128)(2,1)}, s32[24,1024]{1...) while((s32[]{:T(128)}, bf16[24,1024,64]{1,2,0:T(8,128)(2,1)}, ...), condition=%wide.region_12.13_spmd, body=%wide.region_10.12_spmd.sunk | while | flops 682753024 | bytes 34133116 | solution.py:144
  815.1 10.0 fusion.70
  825.1 6.9 fusion.81
  832.1 19.3 %fusion.73 = f32[768,3072]{1,0:T(8,128)} fusion(bf16[2048,3072]{1,0:T(8,128)(2,1)} %add_convert_fusion, f32[2048,768]{0,1:T(8,128)} %copy-done.2, f32[768]{0:T(1024)S(1)} %copy-done.35, f32[768]{0:T(1024)S(1)} %copy-done.33, f32[2048]{0:T(1024)S(1)} %copy-done.20, f32[2048]{0:T(1024)S(1)} %copy-done.15), kind=kOutput, calls=%fused_computation.130 | convolution fusion | flops 9671540736 | bytes 28334080 | tf_op jit(solution)/shard_map/dot_general | solution.py:27
  851.4 16.1 %fusion.66 = f32[3072,768]{0,1:T(8,128)} fusion(bf16[2048,3072]{1,0:T(8,128)(2,1)} %get-tuple-element.289, bf16[2048,768]{0,1:T(8,128)(2,1)} %copy.127, f32[2048]{0:T(1024)S(1)} %copy-done.21), kind=kOutput, calls=%fused_computation.102 | convolution fusion | flops 9668395008 | bytes 25174016 | tf_op jit(solution)/shard_map/dot_general | solution.py:27
  876.5 12.6 %fusion.80 = (f32[768]{0:T(1024)S(1)}, f32[2048,768]{1,0:T(8,128)}) fusion(bf16[2048,2304]{0,1:T(8,128)(2,1)} %copy-done.12, bf16[768,2304]{0,1:T(8,128)(2,1)S(1)} %copy-done.43), kind=kOutput, calls=%fused_computation.136 | convolution fusion | flops 7249329152 | bytes 19270656 | tf_op jit(solution)/shard_map/dot_general | solution.py:33
  889.1 6.7 copy.138
  907.6 16.6 %multiply_convert_fusion.3 = bf16[2048,768]{0,1:T(8,128)(2,1)} fusion(f32[2048,768]{0,1:T(8,128)} %copy-done.2, bf16[2048,3072]{1,0:T(8,128)(2,1)} %get-tuple-element.289, bf16[3072,768]{0,1:T(8,128)(2,1)} %all-gather.14.cloned.1.call-done, f32[2048]{0:T(1024)S(1)} %copy-done.21), kind=kOutput, calls=%fused_computation.97 | convolution fusion | flops 9668395008 | bytes 26746880 | tf_op jit(solution)/shard_map/dot_general | solution.py:23
  924.2 12.6 %reduce-scatter.10.cloned.1.call-done = f32[768,96]{0,1:T(8,128)} async-done(((f32[768,768]{0,1:T(8,128)}), f32[768,96]{0,1:T(8,128)}) %reduce-scatter.10.cloned.1.call-update) | async-done | bytes 294928 | tf_op jit(solution)/shard_map/reduce_scatter | solution.py:160
  938.4 78.4 %reduce-scatter.12.cloned.1.call-done = f32[768,384]{1,0:T(8,128)} async-done(((f32[768,3072]{1,0:T(8,128)}), f32[768,384]{1,0:T(8,128)}) %reduce-scatter.12.cloned.1.call-update) | async-done | bytes 1179664 | tf_op jit(solution)/shard_map/reduce_scatter | solution.py:161
  1019.0 77.9 %reduce-scatter.14.cloned.1.call-done = f32[3072,96]{0,1:T(8,128)} async-done(((f32[3072,768]{0,1:T(8,128)}), f32[3072,96]{0,1:T(8,128)}) %reduce-scatter.14.cloned.1.call-update) | async-done | bytes 1179664 | tf_op jit(solution)/shard_map/reduce_scatter | solution.py:162
  1099.0 8.3 add_convert_fusion.1
  1114.9 18.8 %reduce-scatter.16.cloned.1.call-done = f32[96,4]{1,0:T(8,128)} async-done(((f32[768,4]{1,0:T(8,128)}), f32[96,4]{1,0:T(8,128)}) %reduce-scatter.16.cloned.1.call-update) | async-done | bytes 1552
  1134.6 11.8 psum.28
  1147.0 29.1 %all-gather.16.cloned.1.call-done = bf16[3072,288]{0,1:T(8,128)(2,1)} async-done(((bf16[768,288]{0,1:T(8,128)(2,1)}), bf16[3072,288]{0,1:T(8,128)(2,1)}) %all-gather.16.cloned.1.call-update) | async-done | bytes 1769488 | tf_op jit(solution)/shard_map/all_gather | solution.py:166
  1183.0 56.7 %all-reduce.3.cloned.1.call-done = (bf16[768,96]{0,1:T(8,128)(2,1)}, bf16[768,384]{1,0:T(8,128)(2,1)}, bf16[3072,96]{0,1:T(8,128)(2,1)}) async-done(((bf16[768,96]{0,1:T(8,128)(2,1)}, bf16[768,384]{1,0:T(8,128)(2,1)}, bf16[3072,96]{0,1:T(8,128)(2,1)}), (bf16[768,96]{0,1:T(8,128)(2,1)}, bf16[768,384]{1,0:T(8,128)(2,1)}, bf16[3072,96]{0,1:T(8,128)(2,1)})) %all-reduce.3.cloned.1.call-update) | async-done | bytes 1327120 | tf_op jit(solution)/shard_map/psum | solution.py:167
  (503 shorter events, 636.7 us)
Async XLA Ops:
  7.2 39.4 %all-gather.8.cloned.1.call-start = ((), (), s32[]{:S(2)}) async-start(), calls=%async_computation.5 | async-start | bytes 3981312 | tf_op jit(solution)/shard_map/all_gather | solution.py:97
  7.9 278.0 %all-gather.10.cloned.1.call-start = ((), (), s32[]{:S(2)}) async-start(), calls=%async_computation.6 | async-start | bytes 1327104 | tf_op jit(solution)/shard_map/all_gather | solution.py:98
  8.7 287.6 %all-gather.12.cloned.1.call-start = ((), (), s32[]{:S(2)}) async-start(), calls=%async_computation.7 | async-start | bytes 5308416 | tf_op jit(solution)/shard_map/all_gather | solution.py:99
  9.4 354.5 %all-gather.14.cloned.1.call-start = ((), (), s32[]{:S(2)}) async-start(), calls=%async_computation.8 | async-start | bytes 5308416 | tf_op jit(solution)/shard_map/all_gather | solution.py:100
  10.0 895.5 %reduce-scatter.8.cloned.1.call-start = ((), (), s32[]{:S(2)}) async-start(), calls=%async_computation.9 | async-start | bytes 7962624 | tf_op jit(solution)/shard_map/reduce_scatter | solution.py:159
  15.2 270.6 %copy-start = (bf16[2048,768]{0,1:T(8,128)(2,1)}, bf16[2048,768]{0,1:T(8,128)(2,1)S(1)}, u32[]{:S(2)}) copy-start(bf16[2048,768]{0,1:T(8,128)(2,1)S(1)} %copy.114) | copy-start | bytes 9437188
  15.8 41.5 %copy-start.16 = (f32[2048]{0:T(1024)}, f32[2048]{0:T(1024)S(1)}, u32[]{:S(2)}) copy-start(f32[2048]{0:T(1024)S(1)} %broadcast_multiply_fusion.1) | copy-start | bytes 24580
  17.2 40.0 %copy-start.28 = (f32[2048]{0:T(1024)}, f32[2048]{0:T(1024)S(1)}, u32[]{:S(2)}) copy-start(f32[2048]{0:T(1024)S(1)} %fusion.68) | copy-start | bytes 24580
  27.7 29.5 %copy-start.30 = (f32[768]{0:T(1024)}, f32[768]{0:T(1024)S(1)}, u32[]{:S(2)}) copy-start(f32[768]{0:T(1024)S(1)} %get-tuple-element.245) | copy-start | bytes 9220
  27.7 29.5 %copy-start.37 = (f32[768]{0:T(1024)}, f32[768]{0:T(1024)S(1)}, u32[]{:S(2)}) copy-start(f32[768]{0:T(1024)S(1)} %get-tuple-element.244) | copy-start | bytes 9220
  27.8 263.8 %copy-start.32 = (f32[768]{0:T(1024)}, f32[768]{0:T(1024)S(1)}, u32[]{:S(2)}) copy-start(f32[768]{0:T(1024)S(1)} %get-tuple-element.242) | copy-start | bytes 9220
  27.8 263.8 %copy-start.34 = (f32[768]{0:T(1024)}, f32[768]{0:T(1024)S(1)}, u32[]{:S(2)}) copy-start(f32[768]{0:T(1024)S(1)} %get-tuple-element.243) | copy-start | bytes 9220
  278.0 7.9 copy-start.18
  290.8 5.4 copy-start.14
  296.2 67.7 %copy-start.6 = (bf16[2048,768]{0,1:T(8,128)(2,1)S(1)}, bf16[2048,768]{0,1:T(8,128)(2,1)}, u32[]{:S(2)}) copy-start(bf16[2048,768]{0,1:T(8,128)(2,1)} %copy.127) | copy-start | bytes 9437188
  296.2 67.7 %copy-start.21 = (f32[2048]{0:T(1024)S(1)}, f32[2048]{0:T(1024)}, u32[]{:S(2)}) copy-start(f32[2048]{0:T(1024)} %compare_convert_fusion) | copy-start | bytes 24580
  408.4 6.7 copy-start.15
  408.4 6.7 copy-start.20
  408.4 6.7 copy-start.33
  415.0 6.4 copy-start.27
  415.0 6.4 copy-start.4
  825.1 7.0 copy-start.35
  825.1 111.7 %reduce-scatter.10.cloned.1.call-start = ((), (), s32[]{:S(2)}) async-start(), calls=%async_computation.10 | async-start | bytes 2654208 | tf_op jit(solution)/shard_map/reduce_scatter | solution.py:160
  832.0 184.8 %reduce-scatter.12.cloned.1.call-start = ((), (), s32[]{:S(2)}) async-start(), calls=%async_computation.11 | async-start | bytes 10616832 | tf_op jit(solution)/shard_map/reduce_scatter | solution.py:161
  851.4 245.4 %reduce-scatter.14.cloned.1.call-start = ((), (), s32[]{:S(2)}) async-start(), calls=%async_computation.12 | async-start | bytes 10616832 | tf_op jit(solution)/shard_map/reduce_scatter | solution.py:162
  867.6 266.1 %reduce-scatter.16.cloned.1.call-start = ((), (), s32[]{:S(2)}) async-start(), calls=%async_computation.14 | async-start | bytes 442368
  868.5 6.8 copy-start.10
  868.5 6.8 copy-start.11
  868.5 8.0 copy-start.43
  904.8 271.2 %all-gather.16.cloned.1.call-start = ((), (), s32[]{:S(2)}) async-start(), calls=%async_computation.13 | async-start | bytes 2211840 | tf_op jit(solution)/shard_map/all_gather | solution.py:166
  907.5 191.5 %copy-start.23 = (f32[2048]{0:T(1024)S(1)}, f32[2048]{0:T(1024)}, u32[]{:S(2)}) copy-start(f32[2048]{0:T(1024)} %copy-done.22) | copy-start | bytes 24580
  907.5 332.2 %all-reduce.3.cloned.1.call-start = ((), (), s32[]{:S(2)}) async-start(), calls=%async_computation.15 | async-start | bytes 2654208 | tf_op jit(solution)/shard_map/psum | solution.py:167
  (24 other events, 89.5 us)
Sparse Core Ops, SparseCore 0:
  9.9 36.6 all-gather.7
  48.5 24.0 all-gather.9
  74.5 39.7 all-gather.11
  116.0 38.9 all-gather.13
  825.2 65.4 reduce-scatter.7
  894.3 42.4 reduce-scatter.9
  940.3 76.4 reduce-scatter.11
  1020.3 76.4 reduce-scatter.13
  1099.9 33.8 reduce-scatter.15
  1135.7 40.2 all-gather.15
  1179.2 60.4 all-reduce.2
